TPU v7x, 128 devices: a whole 4x4x4 slice. The times are simulated.
128 devices in a mesh: tm: 4 (over z), cell: 32 (over x, y, core).
Axes of the slice: x: 4, y: 4, z: 4, core: 2. Of those that a mesh axis runs over, the one named last changes fastest.
Arguments:
- cheb_coef: float32 [4, 3, 17, 12288], P('tm', None, None, 'cell'), may hold values from -18 to 18
- obj_cell: int32 [4, 12288, 1], P('tm', 'cell'), may hold values from 0 to 31; in each aligned block of 384 rows (0 to 383, 384 to 767, ..., all dimensions but the last counted through in order) at most 24 rows name the same one
Outputs:
- min_dist_sq: float32 [4, 24576], P('tm', 'cell')
Inputs may be any that keep to these rules, and one draw needn't show every extreme that they name: `obj_cell`: in each subwindow, of the 384 objects of one device (aligned blocks along the objects), at most 24 lie in one cell, and some cell holds exactly 24 of them.
All inputs are finite; a program needn't handle non-finite values.
Results may differ from a plain program's by a relative error of at most 0.0003.
Values sent between devices are 32-bit elements; how exact they have to be, the bound alone decides.
No kernel may reach another device: no remote copies, remote signals or barrier semaphores. Data moves between devices by JAX's collectives and lax.ppermute only.
A program may use at most 128 MiB of HBM per device.

v0:
```python
from functools import reduce

import jax
import jax.numpy as jnp
from jax import lax
from jax.sharding import PartitionSpec as P

DEG1 = 17
SAMP = 64
RIM = 8


clip_level = 25.0


def from_behind(shard, axis, by):
    length = lax.axis_size(axis)
    pairs = [(i, i + by) for i in range(length) if 0 <= i + by < length]
    return lax.ppermute(shard, axis, pairs)


def passed_along(value, axis, steps):
    count = lax.axis_size(axis)
    pairs = [(source, (source + steps) % count) for source in range(count)]
    return lax.ppermute(value, axis, pairs)


def cheb_table(count, degree_plus):
    sample_nodes = (2.0 * jnp.arange(count, dtype=jnp.float32) + 1.0) / count - 1.0
    columns = [jnp.ones_like(sample_nodes), sample_nodes]
    for order in range(2, degree_plus):
        columns.append(2.0 * sample_nodes * columns[-1] - columns[-2])
    return jnp.stack(columns[:degree_plus], axis=1)


def synthesize(coef_three, table):
    return jnp.einsum("sk,ckn->csn", table, coef_three, precision=lax.Precision.HIGHEST)


def slot_ranks(cell_ids):
    positions = jnp.arange(cell_ids.shape[0], dtype=jnp.int32)
    same_cell = cell_ids[:, None] == cell_ids[None, :]
    earlier = positions[None, :] < positions[:, None]
    return jnp.sum((same_cell & earlier).astype(jnp.int32), axis=1)


def screen(left_pos, left_alive, right_pos, right_alive, skip_self):
    total_rows = left_pos.shape[2]
    total_cols = right_pos.shape[2]
    block_rows = min(256, total_rows)

    def one_block(block_num):
        start = block_num * block_rows
        left_block = lax.dynamic_slice_in_dim(left_pos, start, block_rows, 2)
        left_live = lax.dynamic_slice_in_dim(left_alive, start, block_rows, 0)
        row_ids = start + jnp.arange(block_rows, dtype=jnp.int32)
        row_parts = []
        col_parts = []
        for col_start in range(0, total_cols, block_rows):
            right_block = right_pos[:, :, col_start : col_start + block_rows]
            dist_sq = jnp.min(
                jnp.sum(jnp.square(left_block[:, :, :, None] - right_block[:, :, None, :]), axis=0),
                axis=0,
            )
            usable = left_live[:, None] & right_alive[None, col_start : col_start + block_rows]
            if skip_self:
                col_ids = col_start + jnp.arange(block_rows, dtype=jnp.int32)
                usable = usable & (row_ids[:, None] != col_ids[None, :])
            dist_sq = jnp.where(usable, dist_sq, clip_level)
            row_parts.append(jnp.min(dist_sq, axis=1))
            col_parts.append(jnp.min(dist_sq, axis=0))
        return (reduce(jnp.minimum, row_parts), jnp.concatenate(col_parts))

    row_mins, col_mins = lax.map(one_block, jnp.arange(total_rows // block_rows, dtype=jnp.int32))
    return (row_mins.reshape(total_rows), jnp.min(col_mins, axis=0))


def body(cheb_coef, obj_cell):
    table = cheb_table(SAMP, DEG1)
    window_index = lax.axis_index("tm")
    own_coef = cheb_coef[0]
    obj_count = own_coef.shape[2]
    slot_count = 2 * obj_count
    capacity = slot_count // lax.axis_size("cell")
    cell_ids = obj_cell[0, :, 0]
    slots = cell_ids * capacity + slot_ranks(cell_ids)
    alive_send = jnp.zeros((1, 1, slot_count), jnp.int32).at[0, 0, slots].set(1)
    samples = synthesize(own_coef, table)
    rim_in = from_behind(samples[:, SAMP - RIM :], "tm", 1)
    rim_part = jnp.where(window_index == 0, samples[:, :RIM], rim_in)
    extended = jnp.concatenate([rim_part, samples], axis=1)
    send_buffer = jnp.zeros((3, SAMP + RIM, slot_count), jnp.float32).at[:, :, slots].set(extended)
    compact, alive_got = (
        lax.all_to_all(send_buffer, "cell", split_axis=2, concat_axis=2, tiled=True),
        lax.all_to_all(alive_send, "cell", split_axis=2, concat_axis=2, tiled=True),
    )
    alive_rows = alive_got[0, 0] > 0
    next_packed, next_alive = passed_along((compact, alive_got), "cell", -1)
    next_flags = next_alive[0, 0] > 0
    self_rows, unused = screen(compact, alive_rows, compact, alive_rows, True)
    cross_rows, cross_cols = screen(compact, alive_rows, next_packed, next_flags, False)
    prev_packed, prev_alive = passed_along((compact, alive_got), "cell", 1)
    back_rows, unused_cols = screen(compact, alive_rows, prev_packed, prev_alive[0, 0] > 0, False)
    result = jnp.minimum(jnp.minimum(self_rows, cross_rows), back_rows)
    return jnp.minimum(result, clip_level).reshape(1, slot_count)


def solution(mesh):
    in_specs = (P("tm", None, None, "cell"), P("tm", "cell", None))
    out_specs = P("tm", "cell")
    return jax.shard_map(body, mesh=mesh, in_specs=in_specs, out_specs=out_specs, check_vma=False)
```

profile of v0, /device:TPU:0, one launch (start us, length us, event | category | flops | bytes accessed | tf_op | source)
XLA Modules:
  0.0 743.4 jit_solution(8885599722059409866)
XLA Ops:
  1.7 3.9 collective-permute-start
  7.2 2.9 scatter_custom_fusion
  10.2 3.0 reshape.319
  13.2 7.3 all-to-all-start
  21.1 12.0 %scatter_fusion = f32[3,72,768]{1,0,2:T(4,128)S(1)} fusion(f32[3,72,768]{1,0,2:T(4,128)S(1)} %broadcast_in_dim.27, s32[384]{0:T(512)S(1)} %fusion.7, f32[384,3,72]{2,1,0:T(4,128)S(1)} %copy.29), kind=kCustom, calls=%fused_computation.1 | custom fusion | bytes 996864 | tf_op jit(solution)/shard_map/scatter | solution.py:92
  33.1 2.7 reshape.327
  35.9 7.4 all-to-all-start.1
  44.1 13.6 %compare_reduce_fusion.2 = pred[768]{0:T(1024)(128)(4,1)S(1)} fusion(s32[1,1,768]{1,0,2:T(1,128)S(1)} %all-to-all-done), kind=kLoop, calls=%fused_computation.33 | loop fusion | flops 768 | bytes 3840 | tf_op jit(solution)/shard_map/gt | solution.py:97
  57.7 5.0 collective-permute-start.1
  62.7 14.2 %compare_reduce_fusion = pred[768]{0:T(1024)(128)(4,1)} fusion(s32[1,1,768]{1,0,2:T(1,128)S(1)} %collective-permute-done.3), kind=kLoop, calls=%fused_computation.31 | loop fusion | flops 768 | bytes 3840 | tf_op jit(solution)/shard_map/gt | solution.py:103
  77.0 14.4 %compare_reduce_fusion.1 = pred[768]{0:T(1024)(128)(4,1)} fusion(s32[1,1,768]{1,0,2:T(1,128)S(1)} %collective-permute-done.1), kind=kLoop, calls=%fused_computation.32 | loop fusion | flops 768 | bytes 3840 | tf_op jit(solution)/shard_map/gt | solution.py:99
  91.9 2.3 reduce.9
  94.2 1.5 reshape.328
  95.8 1.4 copy.30
  97.1 5.4 collective-permute-start.2
  102.6 213.2 %while.30 = (s32[]{:T(128)}, f32[3,256]{1,0:T(4,128)S(1)}, s32[3]{0:T(128)S(1)}, pred[768]{0:T(1024)(128)(4,1)S(1)}, f32[3,72,768]{2,1,0:T(8,128)}, /*index=5*/s...) while((s32[]{:T(128)}, f32[3,256]{1,0:T(4,128)S(1)}, s32[3]{0:T(128)S(1)}, ...), condition=%wide.region_13.14_spmd, body=%wide.region_3.13_spmd.sunk | while | flops 128188936 | bytes 117713080 | solution.py:74
  105.4 16.7 %multiply_reduce_fusion.16 = f32[72,256,256]{2,1,0:T(8,128)} fusion(f32[3,72,256]{2,1,0:T(8,128)S(1)} %get-tuple-element.449, f32[3,72,256]{2,1,0:T(8,128)S(1)} %get-tuple-element.440), kind=kLoop, calls=%fused_computation.4.clone.1 | loop fusion | flops 37748736 | bytes 19316736 | tf_op jit(solution)/shard_map/while/body/eval_jaxpr/reduce_sum | solution.py:62
  122.0 7.6 %reduce_min.186 = f32[256,256]{1,0:T(8,128)S(1)} reduce(f32[72,256,256]{2,1,0:T(8,128)} %multiply_reduce_fusion.16, f32[]{:T(128)} %constant.25.clone.4..sunk), dimensions={0}, to_apply=%region_5.5 | reduce | flops 4653056 | bytes 19136516 | tf_op jit(solution)/shard_map/while/body/eval_jaxpr/reduce_min | solution.py:61
  129.6 28.4 %multiply_reduce_fusion.15 = (f32[72,256,256]{2,1,0:T(8,128)}, f32[72,256,256]{2,1,0:T(8,128)}) fusion(f32[3,72,256]{2,1,0:T(8,128)S(1)} %get-tuple-element.439, f32[3,72,256]{2,1,0:T(8,128)S(1)} %get-tuple-element.440, f32[3,72,256]{2,1,0:T(8,128)S(1)} %get-tuple-element.441), kind=kLoop, calls=%fused_computation.3.clone.1 | loop fusion | flops 75497472 | bytes 38412288 | tf_op jit(solution)/shard_map/while/body/eval_jaxpr/reduce_sum | solution.py:62
  158.1 7.6 %reduce_min.184 = f32[256,256]{1,0:T(8,128)S(1)} reduce(f32[72,256,256]{2,1,0:T(8,128)} %get-tuple-element.442, f32[]{:T(128)} %constant.25.clone.4..sunk), dimensions={0}, to_apply=%region_8.8 | reduce | flops 4653056 | bytes 19136516 | tf_op jit(solution)/shard_map/while/body/eval_jaxpr/reduce_min | solution.py:61
  165.7 7.6 %reduce_min.185 = f32[256,256]{1,0:T(8,128)S(1)} reduce(f32[72,256,256]{2,1,0:T(8,128)} %get-tuple-element.446, f32[]{:T(128)} %constant.25.clone.4..sunk), dimensions={0}, to_apply=%region_11.11 | reduce | flops 4653056 | bytes 19136516 | tf_op jit(solution)/shard_map/while/body/eval_jaxpr/reduce_min | solution.py:61
  175.1 1.3 fusion.20
  176.5 16.7 %multiply_reduce_fusion.16 = f32[72,256,256]{2,1,0:T(8,128)} fusion(f32[3,72,256]{2,1,0:T(8,128)S(1)} %get-tuple-element.449, f32[3,72,256]{2,1,0:T(8,128)S(1)} %get-tuple-element.440), kind=kLoop, calls=%fused_computation.4.clone.1 | loop fusion | flops 37748736 | bytes 19316736 | tf_op jit(solution)/shard_map/while/body/eval_jaxpr/reduce_sum | solution.py:62
  193.1 7.6 %reduce_min.186 = f32[256,256]{1,0:T(8,128)S(1)} reduce(f32[72,256,256]{2,1,0:T(8,128)} %multiply_reduce_fusion.16, f32[]{:T(128)} %constant.25.clone.4..sunk), dimensions={0}, to_apply=%region_5.5 | reduce | flops 4653056 | bytes 19136516 | tf_op jit(solution)/shard_map/while/body/eval_jaxpr/reduce_min | solution.py:61
  200.7 28.4 %multiply_reduce_fusion.15 = (f32[72,256,256]{2,1,0:T(8,128)}, f32[72,256,256]{2,1,0:T(8,128)}) fusion(f32[3,72,256]{2,1,0:T(8,128)S(1)} %get-tuple-element.439, f32[3,72,256]{2,1,0:T(8,128)S(1)} %get-tuple-element.440, f32[3,72,256]{2,1,0:T(8,128)S(1)} %get-tuple-element.441), kind=kLoop, calls=%fused_computation.3.clone.1 | loop fusion | flops 75497472 | bytes 38412288 | tf_op jit(solution)/shard_map/while/body/eval_jaxpr/reduce_sum | solution.py:62
  229.1 7.6 %reduce_min.184 = f32[256,256]{1,0:T(8,128)S(1)} reduce(f32[72,256,256]{2,1,0:T(8,128)} %get-tuple-element.442, f32[]{:T(128)} %constant.25.clone.4..sunk), dimensions={0}, to_apply=%region_8.8 | reduce | flops 4653056 | bytes 19136516 | tf_op jit(solution)/shard_map/while/body/eval_jaxpr/reduce_min | solution.py:61
  236.7 7.6 %reduce_min.185 = f32[256,256]{1,0:T(8,128)S(1)} reduce(f32[72,256,256]{2,1,0:T(8,128)} %get-tuple-element.446, f32[]{:T(128)} %constant.25.clone.4..sunk), dimensions={0}, to_apply=%region_11.11 | reduce | flops 4653056 | bytes 19136516 | tf_op jit(solution)/shard_map/while/body/eval_jaxpr/reduce_min | solution.py:61
  247.5 16.7 %multiply_reduce_fusion.16 = f32[72,256,256]{2,1,0:T(8,128)} fusion(f32[3,72,256]{2,1,0:T(8,128)S(1)} %get-tuple-element.449, f32[3,72,256]{2,1,0:T(8,128)S(1)} %get-tuple-element.440), kind=kLoop, calls=%fused_computation.4.clone.1 | loop fusion | flops 37748736 | bytes 19316736 | tf_op jit(solution)/shard_map/while/body/eval_jaxpr/reduce_sum | solution.py:62
  264.2 7.6 %reduce_min.186 = f32[256,256]{1,0:T(8,128)S(1)} reduce(f32[72,256,256]{2,1,0:T(8,128)} %multiply_reduce_fusion.16, f32[]{:T(128)} %constant.25.clone.4..sunk), dimensions={0}, to_apply=%region_5.5 | reduce | flops 4653056 | bytes 19136516 | tf_op jit(solution)/shard_map/while/body/eval_jaxpr/reduce_min | solution.py:61
  271.8 28.4 %multiply_reduce_fusion.15 = (f32[72,256,256]{2,1,0:T(8,128)}, f32[72,256,256]{2,1,0:T(8,128)}) fusion(f32[3,72,256]{2,1,0:T(8,128)S(1)} %get-tuple-element.439, f32[3,72,256]{2,1,0:T(8,128)S(1)} %get-tuple-element.440, f32[3,72,256]{2,1,0:T(8,128)S(1)} %get-tuple-element.441), kind=kLoop, calls=%fused_computation.3.clone.1 | loop fusion | flops 75497472 | bytes 38412288 | tf_op jit(solution)/shard_map/while/body/eval_jaxpr/reduce_sum | solution.py:62
  300.2 7.6 %reduce_min.184 = f32[256,256]{1,0:T(8,128)S(1)} reduce(f32[72,256,256]{2,1,0:T(8,128)} %get-tuple-element.442, f32[]{:T(128)} %constant.25.clone.4..sunk), dimensions={0}, to_apply=%region_8.8 | reduce | flops 4653056 | bytes 19136516 | tf_op jit(solution)/shard_map/while/body/eval_jaxpr/reduce_min | solution.py:61
  307.8 7.6 %reduce_min.185 = f32[256,256]{1,0:T(8,128)S(1)} reduce(f32[72,256,256]{2,1,0:T(8,128)} %get-tuple-element.446, f32[]{:T(128)} %constant.25.clone.4..sunk), dimensions={0}, to_apply=%region_11.11 | reduce | flops 4653056 | bytes 19136516 | tf_op jit(solution)/shard_map/while/body/eval_jaxpr/reduce_min | solution.py:61
  316.4 212.8 %while.32 = (s32[]{:T(128)}, f32[3,256]{1,0:T(4,128)S(1)}, s32[3]{0:T(128)S(1)}, pred[768]{0:T(1024)(128)(4,1)S(1)}, pred[768]{0:T(1024)(128)(4,1)S(1)}, /*index...) while((s32[]{:T(128)}, f32[3,256]{1,0:T(4,128)S(1)}, ...), condition=%wide.region_35.36_spmd, body=%wide.region_25.35_spmd.sunk | while | flops 127794952 | bytes 117706952 | solution.py:74
  319.2 16.7 %multiply_reduce_fusion.20 = f32[72,256,256]{2,1,0:T(8,128)} fusion(f32[3,72,256]{2,1,0:T(8,128)S(1)} %get-tuple-element.487, f32[3,72,256]{2,1,0:T(8,128)S(1)} %get-tuple-element.481), kind=kLoop, calls=%fused_computation.25.clone.1 | loop fusion | flops 37748736 | bytes 19316736 | tf_op jit(solution)/shard_map/while/body/eval_jaxpr/reduce_sum | solution.py:62
  335.9 7.6 %reduce_min.194 = f32[256,256]{1,0:T(8,128)S(1)} reduce(f32[72,256,256]{2,1,0:T(8,128)} %multiply_reduce_fusion.20, f32[]{:T(128)} %constant.25.clone.4..sunk.2), dimensions={0}, to_apply=%region_27.27 | reduce | flops 4653056 | bytes 19136516 | tf_op jit(solution)/shard_map/while/body/eval_jaxpr/reduce_min | solution.py:61
  343.5 28.4 %multiply_reduce_fusion.19 = (f32[72,256,256]{2,1,0:T(8,128)}, f32[72,256,256]{2,1,0:T(8,128)}) fusion(f32[3,72,256]{2,1,0:T(8,128)S(1)} %get-tuple-element.480, f32[3,72,256]{2,1,0:T(8,128)S(1)} %get-tuple-element.481, f32[3,72,256]{2,1,0:T(8,128)S(1)} %get-tuple-element.482), kind=kLoop, calls=%fused_computation.24.clone.1 | loop fusion | flops 75497472 | bytes 38412288 | tf_op jit(solution)/shard_map/while/body/eval_jaxpr/reduce_sum | solution.py:62
  371.9 7.6 %reduce_min.192 = f32[256,256]{1,0:T(8,128)S(1)} reduce(f32[72,256,256]{2,1,0:T(8,128)} %get-tuple-element.483, f32[]{:T(128)} %constant.25.clone.4..sunk.2), dimensions={0}, to_apply=%region_30.30 | reduce | flops 4653056 | bytes 19136516 | tf_op jit(solution)/shard_map/while/body/eval_jaxpr/reduce_min | solution.py:61
  379.5 7.6 %reduce_min.193 = f32[256,256]{1,0:T(8,128)S(1)} reduce(f32[72,256,256]{2,1,0:T(8,128)} %get-tuple-element.485, f32[]{:T(128)} %constant.25.clone.4..sunk.2), dimensions={0}, to_apply=%region_33.33 | reduce | flops 4653056 | bytes 19136516 | tf_op jit(solution)/shard_map/while/body/eval_jaxpr/reduce_min | solution.py:61
  390.1 16.7 %multiply_reduce_fusion.20 = f32[72,256,256]{2,1,0:T(8,128)} fusion(f32[3,72,256]{2,1,0:T(8,128)S(1)} %get-tuple-element.487, f32[3,72,256]{2,1,0:T(8,128)S(1)} %get-tuple-element.481), kind=kLoop, calls=%fused_computation.25.clone.1 | loop fusion | flops 37748736 | bytes 19316736 | tf_op jit(solution)/shard_map/while/body/eval_jaxpr/reduce_sum | solution.py:62
  406.8 7.6 %reduce_min.194 = f32[256,256]{1,0:T(8,128)S(1)} reduce(f32[72,256,256]{2,1,0:T(8,128)} %multiply_reduce_fusion.20, f32[]{:T(128)} %constant.25.clone.4..sunk.2), dimensions={0}, to_apply=%region_27.27 | reduce | flops 4653056 | bytes 19136516 | tf_op jit(solution)/shard_map/while/body/eval_jaxpr/reduce_min | solution.py:61
  414.4 28.4 %multiply_reduce_fusion.19 = (f32[72,256,256]{2,1,0:T(8,128)}, f32[72,256,256]{2,1,0:T(8,128)}) fusion(f32[3,72,256]{2,1,0:T(8,128)S(1)} %get-tuple-element.480, f32[3,72,256]{2,1,0:T(8,128)S(1)} %get-tuple-element.481, f32[3,72,256]{2,1,0:T(8,128)S(1)} %get-tuple-element.482), kind=kLoop, calls=%fused_computation.24.clone.1 | loop fusion | flops 75497472 | bytes 38412288 | tf_op jit(solution)/shard_map/while/body/eval_jaxpr/reduce_sum | solution.py:62
  442.8 7.6 %reduce_min.192 = f32[256,256]{1,0:T(8,128)S(1)} reduce(f32[72,256,256]{2,1,0:T(8,128)} %get-tuple-element.483, f32[]{:T(128)} %constant.25.clone.4..sunk.2), dimensions={0}, to_apply=%region_30.30 | reduce | flops 4653056 | bytes 19136516 | tf_op jit(solution)/shard_map/while/body/eval_jaxpr/reduce_min | solution.py:61
  450.4 7.6 %reduce_min.193 = f32[256,256]{1,0:T(8,128)S(1)} reduce(f32[72,256,256]{2,1,0:T(8,128)} %get-tuple-element.485, f32[]{:T(128)} %constant.25.clone.4..sunk.2), dimensions={0}, to_apply=%region_33.33 | reduce | flops 4653056 | bytes 19136516 | tf_op jit(solution)/shard_map/while/body/eval_jaxpr/reduce_min | solution.py:61
  461.0 16.7 %multiply_reduce_fusion.20 = f32[72,256,256]{2,1,0:T(8,128)} fusion(f32[3,72,256]{2,1,0:T(8,128)S(1)} %get-tuple-element.487, f32[3,72,256]{2,1,0:T(8,128)S(1)} %get-tuple-element.481), kind=kLoop, calls=%fused_computation.25.clone.1 | loop fusion | flops 37748736 | bytes 19316736 | tf_op jit(solution)/shard_map/while/body/eval_jaxpr/reduce_sum | solution.py:62
  477.6 7.6 %reduce_min.194 = f32[256,256]{1,0:T(8,128)S(1)} reduce(f32[72,256,256]{2,1,0:T(8,128)} %multiply_reduce_fusion.20, f32[]{:T(128)} %constant.25.clone.4..sunk.2), dimensions={0}, to_apply=%region_27.27 | reduce | flops 4653056 | bytes 19136516 | tf_op jit(solution)/shard_map/while/body/eval_jaxpr/reduce_min | solution.py:61
  485.2 28.4 %multiply_reduce_fusion.19 = (f32[72,256,256]{2,1,0:T(8,128)}, f32[72,256,256]{2,1,0:T(8,128)}) fusion(f32[3,72,256]{2,1,0:T(8,128)S(1)} %get-tuple-element.480, f32[3,72,256]{2,1,0:T(8,128)S(1)} %get-tuple-element.481, f32[3,72,256]{2,1,0:T(8,128)S(1)} %get-tuple-element.482), kind=kLoop, calls=%fused_computation.24.clone.1 | loop fusion | flops 75497472 | bytes 38412288 | tf_op jit(solution)/shard_map/while/body/eval_jaxpr/reduce_sum | solution.py:62
  513.7 7.6 %reduce_min.192 = f32[256,256]{1,0:T(8,128)S(1)} reduce(f32[72,256,256]{2,1,0:T(8,128)} %get-tuple-element.483, f32[]{:T(128)} %constant.25.clone.4..sunk.2), dimensions={0}, to_apply=%region_30.30 | reduce | flops 4653056 | bytes 19136516 | tf_op jit(solution)/shard_map/while/body/eval_jaxpr/reduce_min | solution.py:61
  521.2 7.6 %reduce_min.193 = f32[256,256]{1,0:T(8,128)S(1)} reduce(f32[72,256,256]{2,1,0:T(8,128)} %get-tuple-element.485, f32[]{:T(128)} %constant.25.clone.4..sunk.2), dimensions={0}, to_apply=%region_33.33 | reduce | flops 4653056 | bytes 19136516 | tf_op jit(solution)/shard_map/while/body/eval_jaxpr/reduce_min | solution.py:61
  529.8 212.8 %while.31 = (s32[]{:T(128)}, f32[3,256]{1,0:T(4,128)S(1)}, s32[3]{0:T(128)S(1)}, pred[768]{0:T(1024)(128)(4,1)S(1)}, pred[768]{0:T(1024)(128)(4,1)S(1)}, /*index...) while((s32[]{:T(128)}, f32[3,256]{1,0:T(4,128)S(1)}, ...), condition=%wide.region_24.25_spmd, body=%wide.region_14.24_spmd.sunk | while | flops 127794952 | bytes 117706952 | solution.py:74
  532.6 16.7 %multiply_reduce_fusion.18 = f32[72,256,256]{2,1,0:T(8,128)} fusion(f32[3,72,256]{2,1,0:T(8,128)S(1)} %get-tuple-element.468, f32[3,72,256]{2,1,0:T(8,128)S(1)} %get-tuple-element.462), kind=kLoop, calls=%fused_computation.17.clone.1 | loop fusion | flops 37748736 | bytes 19316736 | tf_op jit(solution)/shard_map/while/body/eval_jaxpr/reduce_sum | solution.py:62
  549.3 7.6 %reduce_min.190 = f32[256,256]{1,0:T(8,128)S(1)} reduce(f32[72,256,256]{2,1,0:T(8,128)} %multiply_reduce_fusion.18, f32[]{:T(128)} %constant.25.clone.4..sunk.1), dimensions={0}, to_apply=%region_16.16 | reduce | flops 4653056 | bytes 19136516 | tf_op jit(solution)/shard_map/while/body/eval_jaxpr/reduce_min | solution.py:61
  556.9 28.4 %multiply_reduce_fusion.17 = (f32[72,256,256]{2,1,0:T(8,128)}, f32[72,256,256]{2,1,0:T(8,128)}) fusion(f32[3,72,256]{2,1,0:T(8,128)S(1)} %get-tuple-element.461, f32[3,72,256]{2,1,0:T(8,128)S(1)} %get-tuple-element.462, f32[3,72,256]{2,1,0:T(8,128)S(1)} %get-tuple-element.463), kind=kLoop, calls=%fused_computation.16.clone.1 | loop fusion | flops 75497472 | bytes 38412288 | tf_op jit(solution)/shard_map/while/body/eval_jaxpr/reduce_sum | solution.py:62
  585.3 7.6 %reduce_min.188 = f32[256,256]{1,0:T(8,128)S(1)} reduce(f32[72,256,256]{2,1,0:T(8,128)} %get-tuple-element.464, f32[]{:T(128)} %constant.25.clone.4..sunk.1), dimensions={0}, to_apply=%region_19.19 | reduce | flops 4653056 | bytes 19136516 | tf_op jit(solution)/shard_map/while/body/eval_jaxpr/reduce_min | solution.py:61
  592.9 7.6 %reduce_min.189 = f32[256,256]{1,0:T(8,128)S(1)} reduce(f32[72,256,256]{2,1,0:T(8,128)} %get-tuple-element.466, f32[]{:T(128)} %constant.25.clone.4..sunk.1), dimensions={0}, to_apply=%region_22.22 | reduce | flops 4653056 | bytes 19136516 | tf_op jit(solution)/shard_map/while/body/eval_jaxpr/reduce_min | solution.py:61
  603.5 16.7 %multiply_reduce_fusion.18 = f32[72,256,256]{2,1,0:T(8,128)} fusion(f32[3,72,256]{2,1,0:T(8,128)S(1)} %get-tuple-element.468, f32[3,72,256]{2,1,0:T(8,128)S(1)} %get-tuple-element.462), kind=kLoop, calls=%fused_computation.17.clone.1 | loop fusion | flops 37748736 | bytes 19316736 | tf_op jit(solution)/shard_map/while/body/eval_jaxpr/reduce_sum | solution.py:62
  620.2 7.6 %reduce_min.190 = f32[256,256]{1,0:T(8,128)S(1)} reduce(f32[72,256,256]{2,1,0:T(8,128)} %multiply_reduce_fusion.18, f32[]{:T(128)} %constant.25.clone.4..sunk.1), dimensions={0}, to_apply=%region_16.16 | reduce | flops 4653056 | bytes 19136516 | tf_op jit(solution)/shard_map/while/body/eval_jaxpr/reduce_min | solution.py:61
  627.8 28.4 %multiply_reduce_fusion.17 = (f32[72,256,256]{2,1,0:T(8,128)}, f32[72,256,256]{2,1,0:T(8,128)}) fusion(f32[3,72,256]{2,1,0:T(8,128)S(1)} %get-tuple-element.461, f32[3,72,256]{2,1,0:T(8,128)S(1)} %get-tuple-element.462, f32[3,72,256]{2,1,0:T(8,128)S(1)} %get-tuple-element.463), kind=kLoop, calls=%fused_computation.16.clone.1 | loop fusion | flops 75497472 | bytes 38412288 | tf_op jit(solution)/shard_map/while/body/eval_jaxpr/reduce_sum | solution.py:62
  656.2 7.6 %reduce_min.188 = f32[256,256]{1,0:T(8,128)S(1)} reduce(f32[72,256,256]{2,1,0:T(8,128)} %get-tuple-element.464, f32[]{:T(128)} %constant.25.clone.4..sunk.1), dimensions={0}, to_apply=%region_19.19 | reduce | flops 4653056 | bytes 19136516 | tf_op jit(solution)/shard_map/while/body/eval_jaxpr/reduce_min | solution.py:61
  663.8 7.6 %reduce_min.189 = f32[256,256]{1,0:T(8,128)S(1)} reduce(f32[72,256,256]{2,1,0:T(8,128)} %get-tuple-element.466, f32[]{:T(128)} %constant.25.clone.4..sunk.1), dimensions={0}, to_apply=%region_22.22 | reduce | flops 4653056 | bytes 19136516 | tf_op jit(solution)/shard_map/while/body/eval_jaxpr/reduce_min | solution.py:61
  674.4 16.7 %multiply_reduce_fusion.18 = f32[72,256,256]{2,1,0:T(8,128)} fusion(f32[3,72,256]{2,1,0:T(8,128)S(1)} %get-tuple-element.468, f32[3,72,256]{2,1,0:T(8,128)S(1)} %get-tuple-element.462), kind=kLoop, calls=%fused_computation.17.clone.1 | loop fusion | flops 37748736 | bytes 19316736 | tf_op jit(solution)/shard_map/while/body/eval_jaxpr/reduce_sum | solution.py:62
  691.1 7.6 %reduce_min.190 = f32[256,256]{1,0:T(8,128)S(1)} reduce(f32[72,256,256]{2,1,0:T(8,128)} %multiply_reduce_fusion.18, f32[]{:T(128)} %constant.25.clone.4..sunk.1), dimensions={0}, to_apply=%region_16.16 | reduce | flops 4653056 | bytes 19136516 | tf_op jit(solution)/shard_map/while/body/eval_jaxpr/reduce_min | solution.py:61
  698.7 28.4 %multiply_reduce_fusion.17 = (f32[72,256,256]{2,1,0:T(8,128)}, f32[72,256,256]{2,1,0:T(8,128)}) fusion(f32[3,72,256]{2,1,0:T(8,128)S(1)} %get-tuple-element.461, f32[3,72,256]{2,1,0:T(8,128)S(1)} %get-tuple-element.462, f32[3,72,256]{2,1,0:T(8,128)S(1)} %get-tuple-element.463), kind=kLoop, calls=%fused_computation.16.clone.1 | loop fusion | flops 75497472 | bytes 38412288 | tf_op jit(solution)/shard_map/while/body/eval_jaxpr/reduce_sum | solution.py:62
  727.1 7.6 %reduce_min.188 = f32[256,256]{1,0:T(8,128)S(1)} reduce(f32[72,256,256]{2,1,0:T(8,128)} %get-tuple-element.464, f32[]{:T(128)} %constant.25.clone.4..sunk.1), dimensions={0}, to_apply=%region_19.19 | reduce | flops 4653056 | bytes 19136516 | tf_op jit(solution)/shard_map/while/body/eval_jaxpr/reduce_min | solution.py:61
  734.7 7.6 %reduce_min.189 = f32[256,256]{1,0:T(8,128)S(1)} reduce(f32[72,256,256]{2,1,0:T(8,128)} %get-tuple-element.466, f32[]{:T(128)} %constant.25.clone.4..sunk.1), dimensions={0}, to_apply=%region_22.22 | reduce | flops 4653056 | bytes 19136516 | tf_op jit(solution)/shard_map/while/body/eval_jaxpr/reduce_min | solution.py:61
  (115 shorter events, 27.0 us)
Async XLA Ops:
  1.7 18.9 %collective-permute-start = (f32[3,8,384]{2,1,0:T(8,128)S(1)}, f32[3,8,384]{2,1,0:T(8,128)S(1)}, u32[]{:S(2)}, u32[]{:S(2)}) collective-permute-start(f32[3,8,384]{2,1,0:T(8,128)S(1)} %slice.66), channel_id=1, source_target_pairs={{0,32},{32,64},{64,96},{1,33},{33,65},{65,97},{2,34},{34,66},{66,9... | collective-permute-start | bytes 110600 | tf_op jit(solution)/shard_map/ppermute | solution.py:19
  13.2 22.7 %all-to-all-start = ((s32[1,1,768]{1,0,2:T(1,128)}), s32[1,1,768]{1,0,2:T(1,128)S(1)}, u32[]{:S(2)}, u32[]{:S(2)}) async-start(s32[1,1,768]{1,0,2:T(1,128)} %reshape.319), calls=%async_computation | async-start | bytes 786432 | tf_op jit(solution)/shard_map/all_to_all | solution.py:95
  35.9 55.5 %all-to-all-start.1 = ((f32[32,1,5184]{2,1,0:T(1,128)}), f32[32,1,5184]{2,1,0:T(1,128)S(1)}, u32[]{:S(2)}, u32[]{:S(2)}) async-start(f32[32,1,5184]{2,1,0:T(1,128)} %reshape.327), calls=%async_computation.1 | async-start | bytes 1343488 | tf_op jit(solution)/shard_map/all_to_all | solution.py:94
  43.2 19.5 %collective-permute-start.3 = (s32[1,1,768]{1,0,2:T(1,128)S(1)}, s32[1,1,768]{1,0,2:T(1,128)S(1)}, u32[]{:S(2)}, u32[]{:S(2)}) collective-permute-start(s32[1,1,768]{1,0,2:T(1,128)S(1)} %all-to-all-done), channel_id=1, source_target_pairs={{0,1},{1,2},{2,3},{3,4},{4,5},{5,6},{6,7},{7,8},{8,9},{9,10},{10,1... | collective-permute-start | bytes 9224 | tf_op jit(solution)/shard_map/ppermute | solution.py:25
  57.7 19.3 %collective-permute-start.1 = (s32[1,1,768]{1,0,2:T(1,128)S(1)}, s32[1,1,768]{1,0,2:T(1,128)S(1)}, u32[]{:S(2)}, u32[]{:S(2)}) collective-permute-start(s32[1,1,768]{1,0,2:T(1,128)S(1)} %all-to-all-done), channel_id=1, source_target_pairs={{0,31},{1,0},{2,1},{3,2},{4,3},{5,4},{6,5},{7,6},{8,7},{9,8},{10,9... | collective-permute-start | bytes 9224 | tf_op jit(solution)/shard_map/ppermute | solution.py:25
  97.1 218.7 %collective-permute-start.4 = (f32[3,72,768]{2,1,0:T(8,128)}, f32[3,72,768]{2,1,0:T(8,128)}, u32[]{:S(2)}, u32[]{:S(2)}) collective-permute-start(f32[3,72,768]{2,1,0:T(8,128)} %copy.30), channel_id=1, source_target_pairs={{0,1},{1,2},{2,3},{3,4},{4,5},{5,6},{6,7},{7,8},{8,9},{9,10},{10,1... | collective-permute-start | bytes 1990664 | tf_op jit(solution)/shard_map/ppermute | solution.py:25
  97.1 432.1 %collective-permute-start.2 = (f32[3,72,768]{2,1,0:T(8,128)}, f32[3,72,768]{2,1,0:T(8,128)}, u32[]{:S(2)}, u32[]{:S(2)}) collective-permute-start(f32[3,72,768]{2,1,0:T(8,128)} %copy.30), channel_id=1, source_target_pairs={{0,31},{1,0},{2,1},{3,2},{4,3},{5,4},{6,5},{7,6},{8,7},{9,8},{10,9... | collective-permute-start | bytes 1990664 | tf_op jit(solution)/shard_map/ppermute | solution.py:25
  102.6 213.3 %copy-start.1 = (pred[768]{0:T(1024)(128)(4,1)S(1)}, pred[768]{0:T(1024)(128)(4,1)}, u32[]{:S(2)}) copy-start(pred[768]{0:T(1024)(128)(4,1)} %compare_reduce_fusion) | copy-start | bytes 2308
  315.8 0.6 copy-start.2
  315.8 213.9 %copy-start = (pred[768]{0:T(1024)(128)(4,1)S(1)}, pred[768]{0:T(1024)(128)(4,1)}, u32[]{:S(2)}) copy-start(pred[768]{0:T(1024)(128)(4,1)} %compare_reduce_fusion.1) | copy-start | bytes 2308
  529.2 0.6 copy-start.4
  529.8 212.8 %copy-start.3 = (f32[3,256]{1,0:T(4,128)S(1)}, f32[3,256]{1,0:T(4,128)}, u32[]{:S(2)}) copy-start(f32[3,256]{1,0:T(4,128)} %copy-done.2) | copy-start | bytes 9220
  529.8 212.8 %copy-start.5 = (f32[3,256]{1,0:T(4,128)S(1)}, f32[3,256]{1,0:T(4,128)}, u32[]{:S(2)}) copy-start(f32[3,256]{1,0:T(4,128)} %copy-done.4) | copy-start | bytes 9220
where the time goes:
time: 750 us; the launch traced here: 743 us
  other arithmetic  660 us (88%)
  local copies, waits for them, and re-layouts  45.1 us (6%)
  starting transfers between devices  29.9 us (4%)
    reduce_sum x18, other arithmetic, one_block(): jnp.sum(jnp.square(left_block[:, :, :, None] - right_block[:, :, None, :]...  406 us
    reduce_min x27, other arithmetic, one_block(): jnp.min(jnp.sum(jnp.square(left_block[:, :, :, None] - right_block[:, :,...  205 us
  transfers between devices with their start and end apart: 7, of which 0 were waited for; matrix products, arithmetic and copies ran while one was open for 65% of the time, Pallas kernels for 0%

commit v1 on v0

v1 whole, which is shorter than its diff:
```python
import functools

import jax
import jax.numpy as jnp
import ml_dtypes
import numpy as np
from jax import lax
from jax.experimental import pallas as pl
from jax.experimental.pallas import tpu as pltpu
from jax.sharding import PartitionSpec as P

DEG1 = 17
SAMP = 64
RIM = 8
CAP = 24
EXT = SAMP + RIM
CLIP = 25.0
FAR = 1.0e9

LANES = 128
RIM_AT = 72
FLAG_AT = 96

PIECES = 32
GROUP = LANES // PIECES
CHUNK = 24
SRC = 256
COLS = 256
UNROLL = 3


def cheb_table():
    nodes = ((2.0 * np.arange(SAMP, dtype=np.float32) + 1.0) / SAMP - 1.0).astype(np.float32)
    columns = [np.ones_like(nodes), nodes]
    for _ in range(2, DEG1):
        columns.append((2.0 * nodes * columns[-1] - columns[-2]).astype(np.float32))
    return np.stack(columns, axis=1)


def rim_tables():
    table = cheb_table()
    return np.stack([table[:RIM], table[SAMP - RIM :]])


def synth_matrix():
    table = cheb_table()
    weights = np.zeros((3 * EXT, LANES), np.float32)
    for c in range(3):
        for s in range(RIM):
            weights[c * EXT + s, RIM_AT + RIM * c + s] = 1.0
        weights[c * EXT + RIM : (c + 1) * EXT, 24 * c : 24 * c + DEG1] = table
    return weights


def selection(left):
    hi, mid, norm, one = 0, 3, 6, 9
    uses = []
    for c in range(3):
        for l, r in ((hi, hi), (hi, mid), (mid, hi), (mid, mid)):
            uses.append((l + c, 1.0) if left else (r + c, -2.0))
    for p in range(3):
        uses.append((norm + p, 1.0) if left else (one, 1.0))
    for p in range(3):
        uses.append((one, 1.0) if left else (norm + p, 1.0))
    matrix = np.zeros((CHUNK * PIECES, SRC), np.float32)
    for t in range(CHUNK):
        for k, (kind, value) in enumerate(uses):
            matrix[t * PIECES + k, kind * CHUNK + (0 if kind == one else t)] = value
    return matrix.astype(ml_dtypes.bfloat16)


def as_piece(value):
    return value.astype(jnp.bfloat16).astype(jnp.float32)


def front_kernel(first_ref, own_ref, prev_ref, cell_ref, table_ref, out_ref, rows_ref):
    count = own_ref.shape[2]
    first = first_ref[0] == 0
    rows_ref[...] = jnp.zeros_like(rows_ref)
    table = jnp.where(first, table_ref[0], table_ref[1])
    for c in range(3):
        own = own_ref[c]
        rows_ref[24 * c : 24 * c + DEG1, :] = own
        source = jnp.where(first, own, prev_ref[c])
        rows_ref[RIM_AT + RIM * c : RIM_AT + RIM * (c + 1), :] = jnp.dot(
            table, source, precision=lax.Precision.HIGHEST, preferred_element_type=jnp.float32
        )
    rows_ref[FLAG_AT : FLAG_AT + 1, :] = jnp.ones((1, count), jnp.float32)
    cell = cell_ref[...].astype(jnp.float32)
    column = jnp.transpose(jnp.broadcast_to(cell, (LANES, count)))
    column = jnp.concatenate([column] * (count // LANES), axis=1)
    before = lax.broadcasted_iota(jnp.int32, (count, count), 0) < lax.broadcasted_iota(jnp.int32, (count, count), 1)
    same = (column == jnp.broadcast_to(cell, (count, count))) & before
    rank = jnp.sum(jnp.where(same, 1.0, 0.0), axis=0, keepdims=True)
    slot = (cell * CAP + rank).astype(jnp.int32)
    slots = out_ref.shape[0]
    chosen = lax.broadcasted_iota(jnp.int32, (slots, count), 0) == jnp.broadcast_to(slot, (slots, count))
    chosen = jnp.where(chosen, 1.0, 0.0).astype(jnp.bfloat16)
    data = jnp.transpose(rows_ref[...])
    total = None
    for _ in range(3):
        piece = data.astype(jnp.bfloat16)
        data = data - piece.astype(jnp.float32)
        term = jnp.dot(chosen, piece, preferred_element_type=jnp.float32)
        total = term if total is None else total + term
    out_ref[...] = total


def operands(packed_ref, synth_ref, right_sel_ref, right_ref, left_sel_ref=None, left_ref=None):
    count = packed_ref.shape[0]
    packed = jnp.transpose(packed_ref[...])
    flag = packed[FLAG_AT : FLAG_AT + 1, :] > 0.5
    track = jnp.dot(synth_ref[...], packed, precision=lax.Precision.HIGHEST, preferred_element_type=jnp.float32)
    axes = [track[c * EXT : (c + 1) * EXT] for c in range(3)]
    hi = [as_piece(a) for a in axes]
    mid = [as_piece(a - h) for a, h in zip(axes, hi)]
    held = [h + m for h, m in zip(hi, mid)]
    norm = held[0] * held[0] + held[1] * held[1] + held[2] * held[2]
    norm = jnp.where(jnp.broadcast_to(flag, norm.shape), norm, FAR)
    norms = []
    for _ in range(3):
        piece = as_piece(norm)
        norm = norm - piece
        norms.append(piece)
    ones = jnp.ones((8, count), jnp.float32)
    zeros = jnp.zeros((SRC - 9 * CHUNK - 8, count), jnp.float32)
    for n in range(EXT // CHUNK):
        rows = slice(n * CHUNK, (n + 1) * CHUNK)
        source = jnp.concatenate([a[rows] for a in hi + mid + norms] + [ones, zeros], axis=0)
        right = jnp.dot(right_sel_ref[...], source.astype(jnp.bfloat16), preferred_element_type=jnp.float32)
        right = right.astype(jnp.bfloat16)
        for t in range(CHUNK):
            right_ref[n * CHUNK + t] = right[t * PIECES : (t + 1) * PIECES]
        if left_ref is not None:
            flipped = jnp.transpose(source).astype(jnp.bfloat16)
            for g in range(CHUNK // GROUP):
                block = jnp.dot(
                    flipped, left_sel_ref[:, g * LANES : (g + 1) * LANES], preferred_element_type=jnp.float32
                )
                left_ref[n * (CHUNK // GROUP) + g] = block.astype(jnp.bfloat16)


def tile_min(left_ref, right_ref, acc_ref, rows, col_start):
    groups = left_ref.shape[0]
    acc_ref[0:rows, :] = jnp.full((rows, COLS), CLIP, jnp.float32)

    def step(it, carry):
        best = acc_ref[0:rows, :]
        for u in range(UNROLL):
            g = it * UNROLL + u
            left = left_ref[g, 0:rows, :]
            for j in range(GROUP):
                block = right_ref[g * GROUP + j, :, pl.ds(col_start, COLS)]
                parts = [block]
                if j > 0:
                    parts = [jnp.zeros((PIECES * j, COLS), jnp.bfloat16)] + parts
                if j < GROUP - 1:
                    parts = parts + [jnp.zeros((PIECES * (GROUP - 1 - j), COLS), jnp.bfloat16)]
                weights = jnp.concatenate(parts, axis=0)
                best = jnp.minimum(best, jnp.dot(left, weights, preferred_element_type=jnp.float32))
        acc_ref[0:rows, :] = best
        return carry

    lax.fori_loop(0, groups // UNROLL, step, 0)


def fold(acc_ref, row_ref, rows):
    acc = acc_ref[0:rows, :]
    half = jnp.minimum(acc[:, :LANES], acc[:, LANES:])
    row_ref[0:rows, :] = jnp.minimum(row_ref[0:rows, :], half)
    return jnp.min(acc, axis=0, keepdims=True)


def self_kernel(packed_ref, synth_ref, left_sel_ref, right_sel_ref, out_ref, left_ref, right_ref, acc_ref, row_ref):
    count = packed_ref.shape[0]
    operands(packed_ref, synth_ref, right_sel_ref, right_ref, left_sel_ref, left_ref)
    row_ref[...] = jnp.full_like(row_ref, CLIP)
    parts = []
    for n in range(count // COLS):
        rows = (n + 1) * COLS
        tile_min(left_ref, right_ref, acc_ref, rows, n * COLS)
        near = acc_ref[rows - COLS : rows, :]
        same = lax.broadcasted_iota(jnp.int32, (COLS, COLS), 0) == lax.broadcasted_iota(jnp.int32, (COLS, COLS), 1)
        acc_ref[rows - COLS : rows, :] = jnp.where(same, CLIP, near)
        parts.append(fold(acc_ref, row_ref, rows))
    by_row = jnp.min(jnp.transpose(row_ref[...]), axis=0, keepdims=True)
    out_ref[...] = jnp.minimum(jnp.concatenate(parts, axis=1), by_row)


def cross_kernel(left_ref, packed_ref, synth_ref, right_sel_ref, row_out_ref, col_out_ref, right_ref, acc_ref, row_ref):
    count = packed_ref.shape[0]
    operands(packed_ref, synth_ref, right_sel_ref, right_ref)
    row_ref[...] = jnp.full_like(row_ref, CLIP)

    def column(n, carry):
        start = pl.multiple_of(n * COLS, COLS)
        tile_min(left_ref, right_ref, acc_ref, count, start)
        col_out_ref[:, pl.ds(start, COLS)] = fold(acc_ref, row_ref, count)
        return carry

    lax.fori_loop(0, count // COLS, column, 0)
    row_out_ref[...] = jnp.min(jnp.transpose(row_ref[...]), axis=0, keepdims=True)


VMEM = pl.BlockSpec(memory_space=pltpu.VMEM)
SMEM = pl.BlockSpec(memory_space=pltpu.SMEM)
PARAMS = pltpu.CompilerParams(vmem_limit_bytes=44 << 20)


def body(cheb_coef, obj_cell):
    own = cheb_coef[0]
    objects = own.shape[2]
    cells = lax.axis_size("cell")
    slots = cells * CAP
    windows = lax.axis_size("tm")
    window = lax.axis_index("tm").astype(jnp.int32).reshape(1)
    prev = lax.ppermute(own, "tm", [(i, i + 1) for i in range(windows - 1)])
    row = jax.ShapeDtypeStruct((1, slots), jnp.float32)
    send = pl.pallas_call(
        front_kernel,
        out_shape=jax.ShapeDtypeStruct((slots, LANES), jnp.float32),
        in_specs=[SMEM, VMEM, VMEM, VMEM, VMEM],
        out_specs=VMEM,
        scratch_shapes=[pltpu.VMEM((LANES, objects), jnp.float32)],
        name="front",
    )(window, own, prev, obj_cell.reshape(1, objects), jnp.asarray(rim_tables()))
    packed = lax.all_to_all(send, "cell", split_axis=0, concat_axis=0, tiled=True)
    following = lax.ppermute(packed, "cell", [((i + 1) % cells, i) for i in range(cells)])
    synth = jnp.asarray(synth_matrix())
    left_sel = jnp.asarray(np.ascontiguousarray(selection(True).T))
    right_sel = jnp.asarray(selection(False))
    left_shape = jax.ShapeDtypeStruct((EXT // GROUP, slots, LANES), jnp.bfloat16)
    right_scratch = pltpu.VMEM((EXT, PIECES, slots), jnp.bfloat16)
    scratch = [right_scratch, pltpu.VMEM((slots, COLS), jnp.float32), pltpu.VMEM((slots, LANES), jnp.float32)]
    cost = pl.CostEstimate(flops=40_000_000_000, bytes_accessed=8_000_000, transcendentals=0)
    own_min, left = pl.pallas_call(
        self_kernel,
        out_shape=(row, left_shape),
        in_specs=[VMEM] * 4,
        out_specs=(VMEM, VMEM),
        scratch_shapes=scratch,
        compiler_params=PARAMS,
        cost_estimate=cost,
        name="self_screen",
    )(packed, synth, left_sel, right_sel)
    row_min, col_min = pl.pallas_call(
        cross_kernel,
        out_shape=(row, row),
        in_specs=[VMEM] * 4,
        out_specs=(VMEM, VMEM),
        scratch_shapes=scratch,
        compiler_params=PARAMS,
        cost_estimate=cost,
        name="cross_screen",
    )(left, following, synth, right_sel)
    back_min = lax.ppermute(col_min, "cell", [(i, (i + 1) % cells) for i in range(cells)])
    result = jnp.minimum(jnp.minimum(own_min, row_min), back_min)
    return jnp.clip(result, 0.0, CLIP)


def solution(mesh):
    in_specs = (P("tm", None, None, "cell"), P("tm", "cell", None))
    return jax.shard_map(body, mesh=mesh, in_specs=in_specs, out_specs=P("tm", "cell"), check_vma=False)
```

time: 750 us -> 89.3 us (0.12)
  other arithmetic: 660 us -> 0.58 us
  Pallas kernels: 0 us -> 51.4 us
  local copies, waits for them, and re-layouts: 45.1 us -> 4.43 us
  starting transfers between devices: 29.9 us -> 6.11 us
  blocking collectives: 0 us -> 17.3 us
  waiting for transfers between devices: 0.02 us -> 8.63 us
    reduce_sum x19 -> x0, other arithmetic: 406 us -> none  [the longest x18 406 us: one_block(): jnp.sum(jnp.square(left_block[:, :, :, None] - right_block[:, :, None, :]...]
    reduce_min x36 -> x0, other arithmetic: 207 us -> none  [the longest x27 205 us: one_block(): jnp.min(jnp.sum(jnp.square(left_block[:, :, :, None] - right_block[:, :,...]
    pallas_call x0 -> x3, Pallas kernels: none -> 51.4 us  [the longest x1 27.3 us: body(): pl.pallas_call(cross_kernel, out_shape=(row, row), in_specs=[VMEM] * 4, o...]
    gt x3 -> x0, other arithmetic: 42.3 us -> none  [the longest x1 14.4 us: body(): next_flags = next_alive[0, 0] > 0]
    scatter x3 -> x0, local copies, waits for them, and re-layouts: 18 us -> none  [the longest x1 12 us: body(): jnp.zeros((3, SAMP + RIM, slot_count), jnp.float32).at[:, :, slots]]
    all_to_all x0 -> x1, blocking collectives: none -> 17.3 us  [body(): lax.all_to_all(send, 'cell', split_axis=0, concat_axis=0, tiled=True)]
    all_to_all x2 -> x0, starting transfers between devices: 14.7 us -> none  [the longest x1 7.38 us: body(): lax.all_to_all(send_buffer, 'cell', split_axis=2, concat_axis=2, tiled=True)]
    slice x19 -> x0, local copies, waits for them, and re-layouts: 12.3 us -> none  [the longest x9 12 us: one_block(): right_block = right_pos[:, :, col_start:col_start + block_rows]]
  transfers between devices with their start and end apart: 7 -> 3, of which waited for: 0 -> 2; matrix products, arithmetic and copies ran while one was open for 65% -> 0% of each run, Pallas kernels for 0% -> 24%
where the time goes in v1:
time: 89.3 us; the launch traced here: 88.5 us
  Pallas kernels  51.4 us (58%)
  blocking collectives  17.3 us (19%)
  waiting for transfers between devices  8.63 us (10%)
  starting transfers between devices  6.11 us (7%)
  local copies, waits for them, and re-layouts  4.43 us (5%)
    pallas_call x1, Pallas kernels, body(): pl.pallas_call(cross_kernel, out_shape=(row, row), in_specs=[VMEM] * 4, o...  27.3 us
    pallas_call x1, Pallas kernels, body(): pl.pallas_call(self_kernel, out_shape=(row, left_shape), in_specs=[VMEM]...  21.5 us
    all_to_all x1, blocking collectives, body(): lax.all_to_all(send, 'cell', split_axis=0, concat_axis=0, tiled=True)  17.3 us
    ppermute x1, waiting for transfers between devices, body(): lax.ppermute(col_min, 'cell', [(i, (i + 1) % cells) for i in range(cells)])  6.33 us
    unnamed x13, local copies, waits for them, and re-layouts  4.43 us
    ppermute x1, starting transfers between devices, body(): prev = lax.ppermute(own, 'tm', [(i, i + 1) for i in range(windows - 1)])  3.91 us
    pallas_call x1, Pallas kernels, body(): pl.pallas_call(front_kernel, out_shape=jax.ShapeDtypeStruct((slots, LANES...  2.63 us
    ppermute x1, waiting for transfers between devices, body(): prev = lax.ppermute(own, 'tm', [(i, i + 1) for i in range(windows - 1)])  2.3 us
  transfers between devices with their start and end apart: 3, of which 2 were waited for; matrix products, arithmetic and copies ran while one was open for 0% of the time, Pallas kernels for 24%

profile of v1, /device:TPU:0, one launch (start us, length us, event | category | flops | bytes accessed | tf_op | source)
XLA Modules:
  0.0 88.5 jit_solution(8807218782661744613)
XLA Ops:
  0.0 0.9 %copy.9 = f32[1,3,17,384]{3,2,0,1:T(8,128)S(1)} copy(f32[1,3,17,384]{3,0,2,1:T(1,128)} %param.6) | data formatting | bytes 156672
  0.9 0.0 copy-start.4
  0.9 3.9 %collective-permute-start = (f32[3,17,384]{2,1,0:T(8,128)S(1)}, f32[3,17,384]{2,1,0:T(8,128)S(1)}, u32[]{:S(2)}, u32[]{:S(2)}) collective-permute-start(f32[3,17,384]{2,1,0:T(8,128)S(1)} %bitcast.10), channel_id=1, source_target_pairs={{0,32},{32,64},{64,96},{1,33},{33,65},{65,97},{2,34},{34,66},{66,9... | collective-permute-start | bytes 235016 | tf_op jit(solution)/shard_map/ppermute | solution.py:217
  4.8 2.3 %collective-permute-done.prev_ref = f32[3,17,384]{2,1,0:T(8,128)S(1)} collective-permute-done((f32[3,17,384]{2,1,0:T(8,128)S(1)}, f32[3,17,384]{2,1,0:T(8,128)S(1)}, u32[]{:S(2)}, u32[]{:S(2)}) %collective-permute-start) | collective-permute-done | bytes 78368 | tf_op jit(solution)/shard_map/ppermute | solution.py:217
  7.1 0.0 copy-start.5
  7.1 0.0 copy-done.4
  7.1 0.6 copy-done.5
  7.8 2.6 %front.1 = f32[768,128]{1,0:T(8,128)} custom-call(s32[1]{0:T(128)} %bitcast.first_ref, f32[3,17,384]{2,1,0:T(8,128)} %bitcast.11, f32[3,17,384]{2,1,0:T(8,128)} %copy-done.5, s32[1,384]{1,0:T(1,128)} %bitcast.12, f32[2,8,17]{2,1,0:T(8,128)} %constant.18.clone.table_ref), custom_call_target="tpu_custom_call" | custom-call | tf_op jit(solution)/shard_map/front/pallas_call | solution.py:219
  10.4 17.3 %all_to_all.11 = f32[32,24,128]{2,1,0:T(8,128)S(1)} all-to-all(f32[32,24,128]{2,1,0:T(8,128)} %bitcast.9), channel_id=1, replica_groups=mesh['tm'=4,'cell'=32] {'cell'}, dimensions={0} | all-to-all | bytes 786432 | tf_op jit(solution)/shard_map/all_to_all | solution.py:227
  27.7 2.1 %collective-permute-start.1 = (f32[768,128]{1,0:T(8,128)S(1)}, f32[768,128]{1,0:T(8,128)S(1)}, u32[]{:S(2)}, u32[]{:S(2)}) collective-permute-start(f32[768,128]{1,0:T(8,128)S(1)} %bitcast.7), channel_id=1, source_target_pairs={{1,0},{2,1},{3,2},{4,3},{5,4},{6,5},{7,6},{8,7},{9,8},{10,9},{11,1... | collective-permute-start | bytes 1179656 | tf_op jit(solution)/shard_map/ppermute | solution.py:228
  29.8 0.0 copy-start
  29.8 1.0 %copy-done = bf16[768,256]{1,0:T(8,128)(2,1)S(1)} copy-done((bf16[768,256]{1,0:T(8,128)(2,1)S(1)}, bf16[768,256]{1,0:T(8,128)(2,1)}, u32[]{:S(2)}) %copy-start) | copy-done | bytes 393240
  30.8 0.0 copy-start.2
  30.8 1.0 %copy-done.2 = bf16[256,768]{1,0:T(8,128)(2,1)S(1)} copy-done((bf16[256,768]{1,0:T(8,128)(2,1)S(1)}, bf16[256,768]{1,0:T(8,128)(2,1)}, u32[]{:S(2)}) %copy-start.2) | copy-done | bytes 393240
  31.8 0.0 copy-start.3
  31.8 0.9 %copy-done.3 = f32[216,128]{1,0:T(8,128)S(1)} copy-done((f32[216,128]{1,0:T(8,128)S(1)}, f32[216,128]{1,0:T(8,128)}, u32[]{:S(2)}) %copy-start.3) | copy-done | bytes 110616
  32.7 0.0 copy-start.1
  32.7 21.5 %self_screen.1 = (f32[1,768]{1,0:T(1,128)S(1)}, bf16[18,768,128]{2,1,0:T(8,128)(2,1)S(1)}) custom-call(f32[768,128]{1,0:T(8,128)S(1)} %bitcast.8, f32[216,128]{1,0:T(8,128)S(1)} %copy-done.3, bf16[256,768]{1,0:T(8,128)(2,1)S(1)} %copy-done.2, bf16[768,256]{1,0:T(8,128)(2,1)S(1)} %copy-done), custom_call_target="tpu_custom_call" | custom-call | flops 40000000000 | bytes 8000000 | tf_op jit(solution)/shard_map/self_screen/pallas_call | solution.py:236
  54.2 0.0 collective-permute-done.1.packed_ref
  54.2 0.0 copy-done.1
  54.2 27.3 %cross_screen.1 = (f32[1,768]{1,0:T(1,128)S(1)}, f32[1,768]{1,0:T(1,128)S(1)}) custom-call(bf16[18,768,128]{2,1,0:T(8,128)(2,1)S(1)} %get-tuple-element.10.left_ref, f32[768,128]{1,0:T(8,128)S(1)} %collective-permute-done.1.packed_ref, f32[216,128]{1,0:T(8,128)S(1)} %copy-done.3, bf16[768,256]{1,0:T(8,128)(2,1)S(1)} %copy-done.1), custom_call_target="tpu_custom_call" | custom-call | flops 40000000000 | bytes 8000000 | tf_op jit(solution)/shard_map/cross_screen/pallas_call | solution.py:246
  81.5 0.1 collective-permute-start.2
  81.6 6.3 %collective-permute-done.2 = f32[1,768]{1,0:T(1,128)S(1)} collective-permute-done((f32[1,768]{1,0:T(1,128)S(1)}, f32[1,768]{1,0:T(1,128)S(1)}, u32[]{:S(2)}, u32[]{:S(2)}) %collective-permute-start.2) | collective-permute-done | bytes 3104 | tf_op jit(solution)/shard_map/ppermute | solution.py:256
  87.9 0.6 minimum_clamp_fusion
Async XLA Ops:
  0.9 6.2 %copy-start.4 = (f32[1,3,17,384]{3,2,0,1:T(8,128)}, f32[1,3,17,384]{3,2,0,1:T(8,128)S(1)}, u32[]{:S(2)}) copy-start(f32[1,3,17,384]{3,2,0,1:T(8,128)S(1)} %copy.9) | copy-start | bytes 235012
  0.9 6.2 %collective-permute-start = (f32[3,17,384]{2,1,0:T(8,128)S(1)}, f32[3,17,384]{2,1,0:T(8,128)S(1)}, u32[]{:S(2)}, u32[]{:S(2)}) collective-permute-start(f32[3,17,384]{2,1,0:T(8,128)S(1)} %bitcast.10), channel_id=1, source_target_pairs={{0,32},{32,64},{64,96},{1,33},{33,65},{65,97},{2,34},{34,66},{66,9... | collective-permute-start | bytes 235016 | tf_op jit(solution)/shard_map/ppermute | solution.py:217
  7.1 0.6 copy-start.5
  27.7 26.5 %collective-permute-start.1 = (f32[768,128]{1,0:T(8,128)S(1)}, f32[768,128]{1,0:T(8,128)S(1)}, u32[]{:S(2)}, u32[]{:S(2)}) collective-permute-start(f32[768,128]{1,0:T(8,128)S(1)} %bitcast.7), channel_id=1, source_target_pairs={{1,0},{2,1},{3,2},{4,3},{5,4},{6,5},{7,6},{8,7},{9,8},{10,9},{11,1... | collective-permute-start | bytes 1179656 | tf_op jit(solution)/shard_map/ppermute | solution.py:228
  29.8 1.0 %copy-start = (bf16[768,256]{1,0:T(8,128)(2,1)S(1)}, bf16[768,256]{1,0:T(8,128)(2,1)}, u32[]{:S(2)}) copy-start(bf16[768,256]{1,0:T(8,128)(2,1)} %constant.21.clone.right_sel_ref) | copy-start | bytes 1179652
  30.8 1.0 %copy-start.2 = (bf16[256,768]{1,0:T(8,128)(2,1)S(1)}, bf16[256,768]{1,0:T(8,128)(2,1)}, u32[]{:S(2)}) copy-start(bf16[256,768]{1,0:T(8,128)(2,1)} %constant.20.clone.left_sel_ref) | copy-start | bytes 1179652
  31.8 0.9 %copy-start.3 = (f32[216,128]{1,0:T(8,128)S(1)}, f32[216,128]{1,0:T(8,128)}, u32[]{:S(2)}) copy-start(f32[216,128]{1,0:T(8,128)} %constant.19.clone.synth_ref) | copy-start | bytes 331780
  32.7 21.5 %copy-start.1 = (bf16[768,256]{1,0:T(8,128)(2,1)S(1)}, bf16[768,256]{1,0:T(8,128)(2,1)}, u32[]{:S(2)}) copy-start(bf16[768,256]{1,0:T(8,128)(2,1)} %constant.21.clone.right_sel_ref) | copy-start | bytes 1179652
  81.5 6.4 %collective-permute-start.2 = (f32[1,768]{1,0:T(1,128)S(1)}, f32[1,768]{1,0:T(1,128)S(1)}, u32[]{:S(2)}, u32[]{:S(2)}) collective-permute-start(f32[1,768]{1,0:T(1,128)S(1)} %get-tuple-element.12), channel_id=1, source_target_pairs={{0,1},{1,2},{2,3},{3,4},{4,5},{5,6},{6,7},{7,8},{8,9},{9,10},{10,1... | collective-permute-start | bytes 9224 | tf_op jit(solution)/shard_map/ppermute | solution.py:256

commit v2 on v1

v2 whole, which is shorter than its diff:
```python
import functools

import jax
import jax.numpy as jnp
import ml_dtypes
import numpy as np
from jax import lax
from jax.experimental import pallas as pl
from jax.experimental.pallas import tpu as pltpu
from jax.sharding import PartitionSpec as P

DEG1 = 17
SAMP = 64
RIM = 8
CAP = 24
EXT = SAMP + RIM
CLIP = 25.0
FAR = 1.0e9

LANES = 128
RIM_AT = 72
FLAG_AT = 96

PIECES = 32
GROUP = LANES // PIECES
CHUNK = 24
PARTS = 2
NORMS = 3
KINDS = 3 * PARTS + NORMS
SRC = 256
COLS = 256
UNROLL = 3
BF16 = jnp.bfloat16


def cheb_table():
    nodes = ((2.0 * np.arange(SAMP, dtype=np.float32) + 1.0) / SAMP - 1.0).astype(np.float32)
    columns = [np.ones_like(nodes), nodes]
    for _ in range(2, DEG1):
        columns.append((2.0 * nodes * columns[-1] - columns[-2]).astype(np.float32))
    return np.stack(columns, axis=1)


def rim_tables():
    table = cheb_table()
    return np.stack([table[:RIM], table[SAMP - RIM :]])


def synth_matrix():
    table = cheb_table()
    weights = np.zeros((3 * EXT, LANES), np.float32)
    for c in range(3):
        for s in range(RIM):
            weights[c * EXT + s, RIM_AT + RIM * c + s] = 1.0
        weights[c * EXT + RIM : (c + 1) * EXT, 24 * c : 24 * c + DEG1] = table
    return weights


def selection(left):
    one = KINDS
    uses = []
    for i in range(PARTS):
        for j in range(PARTS):
            for c in range(3):
                uses.append((3 * i + c, 1.0) if left else (3 * j + c, -1.0))
    for n in range(NORMS):
        uses.append((3 * PARTS + n, 1.0) if left else (one, 1.0))
    for n in range(NORMS):
        uses.append((one, 1.0) if left else (3 * PARTS + n, 1.0))
    matrix = np.zeros((CHUNK * PIECES, SRC), np.float32)
    for t in range(CHUNK):
        for k, (kind, value) in enumerate(uses):
            matrix[t * PIECES + k, kind * CHUNK + (0 if kind == one else t)] = value
    return matrix.astype(ml_dtypes.bfloat16)


def split(value, count):
    pieces = []
    for _ in range(count):
        piece = value.astype(BF16).astype(jnp.float32)
        value = value - piece
        pieces.append(piece)
    return pieces, value


def place_kernel(cell_ref, out_ref):
    slots, count = out_ref.shape
    cell = cell_ref[...].astype(jnp.float32)
    column = jnp.transpose(jnp.broadcast_to(cell, (LANES, count)))
    column = jnp.concatenate([column] * (count // LANES), axis=1)
    before = lax.broadcasted_iota(jnp.int32, (count, count), 0) < lax.broadcasted_iota(jnp.int32, (count, count), 1)
    same = (column == jnp.broadcast_to(cell, (count, count))) & before
    rank = jnp.sum(jnp.where(same, 1.0, 0.0), axis=0, keepdims=True)
    slot = (cell * CAP + rank).astype(jnp.int32)
    chosen = lax.broadcasted_iota(jnp.int32, (slots, count), 0) == jnp.broadcast_to(slot, (slots, count))
    out_ref[...] = jnp.where(chosen, 1.0, 0.0).astype(BF16)


def front_kernel(first_ref, own_ref, prev_ref, chosen_ref, table_ref, out_ref, rows_ref):
    count = chosen_ref.shape[1]
    blocks = count // LANES
    first = first_ref[0] == 0
    rows_ref[...] = jnp.zeros_like(rows_ref)
    table = jnp.where(first, table_ref[0], table_ref[1])
    for c in range(3):
        for n in range(blocks):
            lanes = slice(n * LANES, (n + 1) * LANES)
            rows = pl.ds(c * DEG1 * blocks + n, DEG1, stride=blocks)
            own = own_ref[rows, :]
            rows_ref[24 * c : 24 * c + DEG1, lanes] = own
            source = jnp.where(first, own, prev_ref[rows, :])
            rows_ref[RIM_AT + RIM * c : RIM_AT + RIM * (c + 1), lanes] = jnp.dot(
                table, source, precision=lax.Precision.HIGHEST, preferred_element_type=jnp.float32
            )
    rows_ref[FLAG_AT : FLAG_AT + 1, :] = jnp.ones((1, count), jnp.float32)
    data = jnp.transpose(rows_ref[...])
    total = None
    for _ in range(3):
        piece = data.astype(BF16)
        data = data - piece.astype(jnp.float32)
        term = jnp.dot(chosen_ref[...], piece, preferred_element_type=jnp.float32)
        total = term if total is None else total + term
    out_ref[...] = total


def fetched(sources, targets, sem):
    copies = [pltpu.make_async_copy(s, t, sem.at[i]) for i, (s, t) in enumerate(zip(sources, targets))]
    for copy in copies:
        copy.start()
    return copies


def operands(packed_ref, synth_ref, right_sel_ref, right_ref, copies, left_sel_ref=None, left_ref=None):
    count = packed_ref.shape[0]
    packed = jnp.transpose(packed_ref[...])
    flag = packed[FLAG_AT : FLAG_AT + 1, :] > 0.5
    for copy in copies:
        copy.wait()
    track = jnp.dot(synth_ref[...], packed, precision=lax.Precision.HIGHEST, preferred_element_type=jnp.float32)
    parts = [[], [], []]
    norm = None
    for c in range(3):
        axis = track[c * EXT : (c + 1) * EXT]
        parts[c], rest = split(axis, PARTS)
        held = axis - rest
        norm = held * held if norm is None else norm + held * held
    norm = jnp.where(jnp.broadcast_to(flag, norm.shape), 0.5 * norm, FAR)
    kinds = [parts[c][i] for i in range(PARTS) for c in range(3)] + split(norm, NORMS)[0]
    ones = jnp.ones((8, count), jnp.float32)
    zeros = jnp.zeros((SRC - KINDS * CHUNK - 8, count), jnp.float32)
    for n in range(EXT // CHUNK):
        rows = slice(n * CHUNK, (n + 1) * CHUNK)
        source = jnp.concatenate([k[rows] for k in kinds] + [ones, zeros], axis=0)
        right = jnp.dot(right_sel_ref[...], source.astype(BF16), preferred_element_type=jnp.float32).astype(BF16)
        for t in range(CHUNK):
            right_ref[n * CHUNK + t] = right[t * PIECES : (t + 1) * PIECES]
        if left_ref is not None:
            flipped = jnp.transpose(source).astype(BF16)
            for g in range(CHUNK // GROUP):
                block = jnp.dot(
                    flipped, left_sel_ref[:, g * LANES : (g + 1) * LANES], preferred_element_type=jnp.float32
                )
                left_ref[n * (CHUNK // GROUP) + g] = block.astype(BF16)


def tile_min(left_ref, right_ref, acc_ref, rows, col_start):
    groups = left_ref.shape[0]
    acc_ref[0:rows, :] = jnp.full((rows, COLS), CLIP, jnp.float32)

    def step(it, carry):
        best = acc_ref[0:rows, :]
        for u in range(UNROLL):
            g = it * UNROLL + u
            left = left_ref[g, 0:rows, :]
            for j in range(GROUP):
                block = right_ref[g * GROUP + j, :, pl.ds(col_start, COLS)]
                parts = [block]
                if j > 0:
                    parts = [jnp.zeros((PIECES * j, COLS), BF16)] + parts
                if j < GROUP - 1:
                    parts = parts + [jnp.zeros((PIECES * (GROUP - 1 - j), COLS), BF16)]
                weights = jnp.concatenate(parts, axis=0)
                best = jnp.minimum(best, jnp.dot(left, weights, preferred_element_type=jnp.float32))
        acc_ref[0:rows, :] = best
        return carry

    lax.fori_loop(0, groups // UNROLL, step, 0)


def fold(acc_ref, row_ref, rows):
    acc = acc_ref[0:rows, :]
    half = jnp.minimum(acc[:, :LANES], acc[:, LANES:])
    row_ref[0:rows, :] = jnp.minimum(row_ref[0:rows, :], half)
    return jnp.min(acc, axis=0, keepdims=True)


def finished(half):
    return jnp.clip(2.0 * half, 0.0, CLIP)


def prepare_kernel(
    packed_ref, synth_hbm, left_sel_hbm, right_sel_hbm, left_ref, right_ref, synth_ref, left_sel_ref, right_sel_ref, sem
):
    copies = fetched((synth_hbm, left_sel_hbm, right_sel_hbm), (synth_ref, left_sel_ref, right_sel_ref), sem)
    operands(packed_ref, synth_ref, right_sel_ref, right_ref, copies, left_sel_ref, left_ref)


def self_kernel(left_ref, right_ref, cross_ref, out_ref, acc_ref, row_ref):
    count = left_ref.shape[1]
    row_ref[...] = jnp.full_like(row_ref, CLIP)
    parts = []
    for n in range(count // COLS):
        rows = (n + 1) * COLS
        tile_min(left_ref, right_ref, acc_ref, rows, n * COLS)
        near = acc_ref[rows - COLS : rows, :]
        same = lax.broadcasted_iota(jnp.int32, (COLS, COLS), 0) == lax.broadcasted_iota(jnp.int32, (COLS, COLS), 1)
        acc_ref[rows - COLS : rows, :] = jnp.where(same, CLIP, near)
        parts.append(fold(acc_ref, row_ref, rows))
    by_row = jnp.min(jnp.transpose(row_ref[...]), axis=0, keepdims=True)
    best = jnp.minimum(jnp.concatenate(parts, axis=1), by_row)
    out_ref[...] = jnp.minimum(finished(best), cross_ref[...])


def cross_kernel(
    left_ref, packed_ref, synth_hbm, right_sel_hbm, row_out_ref, col_out_ref, right_ref, acc_ref, row_ref, synth_ref,
    right_sel_ref, sem
):
    count = packed_ref.shape[0]
    copies = fetched((synth_hbm, right_sel_hbm), (synth_ref, right_sel_ref), sem)
    operands(packed_ref, synth_ref, right_sel_ref, right_ref, copies)
    row_ref[...] = jnp.full_like(row_ref, CLIP)

    def column(n, carry):
        start = pl.multiple_of(n * COLS, COLS)
        tile_min(left_ref, right_ref, acc_ref, count, start)
        col_out_ref[:, pl.ds(start, COLS)] = finished(fold(acc_ref, row_ref, count))
        return carry

    lax.fori_loop(0, count // COLS, column, 0)
    row_out_ref[...] = finished(jnp.min(jnp.transpose(row_ref[...]), axis=0, keepdims=True))


VMEM = pl.BlockSpec(memory_space=pltpu.VMEM)
SMEM = pl.BlockSpec(memory_space=pltpu.SMEM)
ANY = pl.BlockSpec(memory_space=pl.ANY)


def call(kernel, name, out_shape, in_specs, scratch, vmem, flops):
    return pl.pallas_call(
        kernel,
        out_shape=out_shape,
        in_specs=in_specs,
        out_specs=jax.tree.map(lambda _: VMEM, out_shape),
        scratch_shapes=scratch,
        compiler_params=pltpu.CompilerParams(vmem_limit_bytes=vmem << 20),
        cost_estimate=pl.CostEstimate(flops=flops, bytes_accessed=4_000_000, transcendentals=0),
        name=name,
    )


def body(cheb_coef, obj_cell):
    objects = cheb_coef.shape[3]
    own = cheb_coef.reshape(-1, LANES)
    cells = lax.axis_size("cell")
    slots = cells * CAP
    windows = lax.axis_size("tm")
    window = lax.axis_index("tm").astype(jnp.int32).reshape(1)
    prev = lax.ppermute(own, "tm", [(i, i + 1) for i in range(windows - 1)])
    row = jax.ShapeDtypeStruct((1, slots), jnp.float32)
    chosen = call(
        place_kernel, "place", jax.ShapeDtypeStruct((slots, objects), BF16), [VMEM], [], 8, 2_000_000_000
    )(obj_cell.reshape(1, objects))
    send = call(
        front_kernel,
        "front",
        jax.ShapeDtypeStruct((slots, LANES), jnp.float32),
        [SMEM, VMEM, VMEM, VMEM, VMEM],
        [pltpu.VMEM((LANES, objects), jnp.float32)],
        8,
        2_000_000_000,
    )(window, own, prev, chosen, jnp.asarray(rim_tables()))
    packed = lax.all_to_all(send, "cell", split_axis=0, concat_axis=0, tiled=True)
    following = lax.ppermute(packed, "cell", [((i + 1) % cells, i) for i in range(cells)])
    synth = jnp.asarray(synth_matrix())
    left_sel = jnp.asarray(np.ascontiguousarray(selection(True).T))
    right_sel = jnp.asarray(selection(False))
    left_shape = jax.ShapeDtypeStruct((EXT // GROUP, slots, LANES), BF16)
    right_shape = jax.ShapeDtypeStruct((EXT, PIECES, slots), BF16)
    synth_scratch = pltpu.VMEM(synth.shape, jnp.float32)
    left_sel_scratch = pltpu.VMEM(left_sel.shape, BF16)
    right_sel_scratch = pltpu.VMEM(right_sel.shape, BF16)
    minima = [pltpu.VMEM((slots, COLS), jnp.float32), pltpu.VMEM((slots, LANES), jnp.float32)]
    left, right = call(
        prepare_kernel,
        "prepare",
        (left_shape, right_shape),
        [VMEM, ANY, ANY, ANY],
        [synth_scratch, left_sel_scratch, right_sel_scratch, pltpu.SemaphoreType.DMA((3,))],
        24,
        6_000_000_000,
    )(packed, synth, left_sel, right_sel)
    row_min, col_min = call(
        cross_kernel,
        "cross_screen",
        (row, row),
        [VMEM, VMEM, ANY, ANY],
        [pltpu.VMEM(right_shape.shape, BF16)]
        + minima
        + [synth_scratch, right_sel_scratch, pltpu.SemaphoreType.DMA((2,))],
        32,
        20_000_000_000,
    )(left, following, synth, right_sel)
    back_min = lax.ppermute(col_min, "cell", [(i, (i + 1) % cells) for i in range(cells)])
    own_min = call(self_kernel, "self_screen", row, [VMEM] * 3, minima, 24, 15_000_000_000)(left, right, row_min)
    return jnp.minimum(own_min, back_min)


def solution(mesh):
    in_specs = (P("tm", None, None, "cell"), P("tm", "cell", None))
    return jax.shard_map(body, mesh=mesh, in_specs=in_specs, out_specs=P("tm", "cell"), check_vma=False)
```

time: 89.3 us -> 80.6 us (0.903)
  waiting for transfers between devices: 8.63 us -> 1.92 us
  local copies, waits for them, and re-layouts: 4.43 us -> 0.7 us
  other arithmetic: 0.58 us -> 1.66 us
    ppermute x1, waiting for transfers between devices: 6.33 us -> 0.01 us  [body(): lax.ppermute(col_min, 'cell', [(i, (i + 1) % cells) for i in range(cells)])]
    unnamed x13 -> x10, local copies, waits for them, and re-layouts: 4.43 us -> 0.69 us
    ppermute x1, waiting for transfers between devices: 2.3 us -> 0.95 us  [body(): prev = lax.ppermute(own, 'tm', [(i, i + 1) for i in range(windows - 1)])]
    unnamed x0 -> x1, other arithmetic: none -> 1.08 us
    ppermute x1, waiting for transfers between devices: 0.01 us -> 0.97 us  [body(): lax.ppermute(packed, 'cell', [((i + 1) % cells, i) for i in range(cells)])]
    pallas_call x3 -> x5, Pallas kernels: 51.4 us -> 51.3 us  [the longest x1 27.7 us: body(): call(cross_kernel, 'cross_screen', (row, row), [VMEM, VMEM, ANY, ANY], [p...]
  transfers between devices with their start and end apart: 3 -> 3, of which waited for: 2 -> 2; matrix products, arithmetic and copies ran while one was open for 0% -> 0% of each run, Pallas kernels for 24% -> 28%
where the time goes in v2:
time: 80.6 us; the launch traced here: 79.4 us
  Pallas kernels  51.3 us (64%)
  blocking collectives  17.1 us (21%)
  starting transfers between devices  6.69 us (8%)
  waiting for transfers between devices  1.92 us (2%)
  other arithmetic  1.66 us (2%)
    pallas_call x1, Pallas kernels, body(): call(cross_kernel, 'cross_screen', (row, row), [VMEM, VMEM, ANY, ANY], [p...  27.7 us
    pallas_call x1, Pallas kernels, body(): call(self_kernel, 'self_screen', row, [VMEM] * 3, minima, 24, 15000000000)  17.9 us
    all_to_all x1, blocking collectives, body(): lax.all_to_all(send, 'cell', split_axis=0, concat_axis=0, tiled=True)  17.1 us
    pallas_call x1, Pallas kernels, body(): call(prepare_kernel, 'prepare', (left_shape, right_shape), [VMEM, ANY, AN...  4.31 us
    ppermute x1, starting transfers between devices, body(): prev = lax.ppermute(own, 'tm', [(i, i + 1) for i in range(windows - 1)])  3.91 us
    ppermute x1, starting transfers between devices, body(): lax.ppermute(packed, 'cell', [((i + 1) % cells, i) for i in range(cells)])  2.13 us
  transfers between devices with their start and end apart: 3, of which 2 were waited for; matrix products, arithmetic and copies ran while one was open for 0% of the time, Pallas kernels for 28%

profile of v2, /device:TPU:0, one launch (start us, length us, event | category | flops | bytes accessed | tf_op | source)
XLA Modules:
  0.0 79.4 jit_solution(9123054326128990273)
XLA Ops:
  0.0 1.1 %reduce = f32[3,17,384]{2,1,0:T(8,128)S(1)} reduce(f32[1,3,17,384]{3,0,2,1:T(1,128)} %param.6, f32[]{:T(128)} %constant.20), dimensions={0}, to_apply=%param.6.reduce_sub_computation | reduce | bytes 156676 | tf_op args[0]
  1.1 3.9 %collective-permute-start = (f32[153,128]{1,0:T(8,128)S(1)}, f32[153,128]{1,0:T(8,128)S(1)}, u32[]{:S(2)}, u32[]{:S(2)}) collective-permute-start(f32[153,128]{1,0:T(8,128)S(1)} %reshape.12.own_ref), channel_id=1, source_target_pairs={{0,32},{32,64},{64,96},{1,33},{33,65},{65,97},{2,34},{34,66},{66,9... | collective-permute-start | bytes 235016 | tf_op jit(solution)/shard_map/ppermute | solution.py:268
  5.0 0.0 copy-start
  5.0 0.7 copy-done
  5.7 0.0 copy-start.4
  5.7 0.4 place.1.chosen_ref
  6.1 0.9 %collective-permute-done.prev_ref = f32[153,128]{1,0:T(8,128)S(1)} collective-permute-done((f32[153,128]{1,0:T(8,128)S(1)}, f32[153,128]{1,0:T(8,128)S(1)}, u32[]{:S(2)}, u32[]{:S(2)}) %collective-permute-start) | collective-permute-done | bytes 78368 | tf_op jit(solution)/shard_map/ppermute | solution.py:268
  7.1 0.0 copy-done.4
  7.1 0.0 copy-start.1
  7.1 0.0 copy-start.2
  7.1 0.0 copy-start.3
  7.1 1.0 %front.1 = f32[768,128]{1,0:T(8,128)S(1)} custom-call(s32[1]{0:T(128)} %bitcast.first_ref, f32[153,128]{1,0:T(8,128)S(1)} %reshape.12.own_ref, f32[153,128]{1,0:T(8,128)S(1)} %collective-permute-done.prev_ref, bf16[768,384]{1,0:T(8,128)(2,1)S(1)} %place.1.chosen_ref, f32[2,8,17]{2,1,0:T(8,128)S(1)} %copy-done.4), custom_call_target="tpu_custom_call" | custom-call | flops 2000000000 | bytes 4000000 | tf_op jit(solution)/shard_map/front/pallas_call | solution.py:273
  8.0 17.1 %all_to_all.11 = f32[32,24,128]{2,1,0:T(8,128)S(1)} all-to-all(f32[32,24,128]{2,1,0:T(8,128)S(1)} %bitcast.6), channel_id=1, replica_groups=mesh['tm'=4,'cell'=32] {'cell'}, dimensions={0} | all-to-all | bytes 786432 | tf_op jit(solution)/shard_map/all_to_all | solution.py:282
  25.1 2.1 %collective-permute-start.1 = (f32[768,128]{1,0:T(8,128)S(1)}, f32[768,128]{1,0:T(8,128)S(1)}, u32[]{:S(2)}, u32[]{:S(2)}) collective-permute-start(f32[768,128]{1,0:T(8,128)S(1)} %bitcast.4), channel_id=1, source_target_pairs={{1,0},{2,1},{3,2},{4,3},{5,4},{6,5},{7,6},{8,7},{9,8},{10,9},{11,1... | collective-permute-start | bytes 1179656 | tf_op jit(solution)/shard_map/ppermute | solution.py:283
  27.2 0.0 copy-done.1
  27.2 0.0 copy-done.2
  27.2 0.0 copy-done.3
  27.2 4.3 %prepare.1 = (bf16[18,768,128]{2,1,0:T(8,128)(2,1)S(1)}, bf16[72,32,768]{2,1,0:T(8,128)(2,1)S(1)}) custom-call(f32[768,128]{1,0:T(8,128)S(1)} %bitcast.5, f32[216,128]{1,0:T(8,128)S(1)} %copy-done.3, bf16[256,768]{1,0:T(8,128)(2,1)S(1)} %copy-done.2, bf16[768,256]{1,0:T(8,128)(2,1)S(1)} %copy-done.1), custom_call_target="tpu_custom_call" | custom-call | flops 6000000000 | bytes 4000000 | tf_op jit(solution)/shard_map/prepare/pallas_call | solution.py:293
  31.6 1.0 %collective-permute-done.1.packed_ref = f32[768,128]{1,0:T(8,128)S(1)} collective-permute-done((f32[768,128]{1,0:T(8,128)S(1)}, f32[768,128]{1,0:T(8,128)S(1)}, u32[]{:S(2)}, u32[]{:S(2)}) %collective-permute-start.1) | collective-permute-done | bytes 393248 | tf_op jit(solution)/shard_map/ppermute | solution.py:283
  32.5 27.7 %cross_screen.1 = (f32[1,768]{1,0:T(1,128)S(1)}, f32[1,768]{1,0:T(1,128)S(1)}) custom-call(bf16[18,768,128]{2,1,0:T(8,128)(2,1)S(1)} %get-tuple-element.9.left_ref, f32[768,128]{1,0:T(8,128)S(1)} %collective-permute-done.1.packed_ref, f32[216,128]{1,0:T(8,128)S(1)} %copy-done.3, bf16[768,256]{1,0:T(8,128)(2,1)S(1)} %copy-done.1), custom_call_target="tpu_custom_call" | custom-call | flops 20000000000 | bytes 4000000 | tf_op jit(solution)/shard_map/cross_screen/pallas_call | solution.py:302
  60.3 0.7 collective-permute-start.2
  60.9 17.9 %self_screen.1 = f32[1,768]{1,0:T(1,128)S(1)} custom-call(bf16[18,768,128]{2,1,0:T(8,128)(2,1)S(1)} %get-tuple-element.9.left_ref, bf16[72,32,768]{2,1,0:T(8,128)(2,1)S(1)} %get-tuple-element.10.right_ref, f32[1,768]{1,0:T(1,128)S(1)} %get-tuple-element.11.cross_ref), custom_call_target="tpu_custom_call" | custom-call | flops 15000000512 | bytes 4000000 | tf_op jit(solution)/shard_map/self_screen/pallas_call | solution.py:314
  78.8 0.0 collective-permute-done.2
  78.9 0.6 min.3
  (1 shorter events, 0.0 us)
Async XLA Ops:
  1.1 6.0 %collective-permute-start = (f32[153,128]{1,0:T(8,128)S(1)}, f32[153,128]{1,0:T(8,128)S(1)}, u32[]{:S(2)}, u32[]{:S(2)}) collective-permute-start(f32[153,128]{1,0:T(8,128)S(1)} %reshape.12.own_ref), channel_id=1, source_target_pairs={{0,32},{32,64},{64,96},{1,33},{33,65},{65,97},{2,34},{34,66},{66,9... | collective-permute-start | bytes 235016 | tf_op jit(solution)/shard_map/ppermute | solution.py:268
  5.0 0.7 copy-start
  5.7 1.4 %copy-start.4 = (f32[2,8,17]{2,1,0:T(8,128)S(1)}, f32[2,8,17]{2,1,0:T(8,128)}, u32[]{:S(2)}) copy-start(f32[2,8,17]{2,1,0:T(8,128)} %constant.14.clone.table_ref) | copy-start | bytes 3268
  7.1 20.2 %copy-start.1 = (bf16[768,256]{1,0:T(8,128)(2,1)S(1)}, bf16[768,256]{1,0:T(8,128)(2,1)}, u32[]{:S(2)}) copy-start(bf16[768,256]{1,0:T(8,128)(2,1)} %constant.17.clone.right_sel_hbm) | copy-start | bytes 1179652
  7.1 20.2 %copy-start.2 = (bf16[256,768]{1,0:T(8,128)(2,1)S(1)}, bf16[256,768]{1,0:T(8,128)(2,1)}, u32[]{:S(2)}) copy-start(bf16[256,768]{1,0:T(8,128)(2,1)} %constant.16.clone.left_sel_hbm) | copy-start | bytes 1179652
  7.1 20.2 %copy-start.3 = (f32[216,128]{1,0:T(8,128)S(1)}, f32[216,128]{1,0:T(8,128)}, u32[]{:S(2)}) copy-start(f32[216,128]{1,0:T(8,128)} %constant.15.clone.synth_hbm) | copy-start | bytes 331780
  25.1 7.4 %collective-permute-start.1 = (f32[768,128]{1,0:T(8,128)S(1)}, f32[768,128]{1,0:T(8,128)S(1)}, u32[]{:S(2)}, u32[]{:S(2)}) collective-permute-start(f32[768,128]{1,0:T(8,128)S(1)} %bitcast.4), channel_id=1, source_target_pairs={{1,0},{2,1},{3,2},{4,3},{5,4},{6,5},{7,6},{8,7},{9,8},{10,9},{11,1... | collective-permute-start | bytes 1179656 | tf_op jit(solution)/shard_map/ppermute | solution.py:283
  60.3 18.6 %collective-permute-start.2 = (f32[1,768]{1,0:T(1,128)S(1)}, f32[1,768]{1,0:T(1,128)S(1)}, u32[]{:S(2)}, u32[]{:S(2)}) collective-permute-start(f32[1,768]{1,0:T(1,128)S(1)} %get-tuple-element.12), channel_id=1, source_target_pairs={{0,1},{1,2},{2,3},{3,4},{4,5},{5,6},{6,7},{7,8},{8,9},{9,10},{10,1... | collective-permute-start | bytes 9224 | tf_op jit(solution)/shard_map/ppermute | solution.py:313
